TPU v7x, 32 devices: a whole 2x2x4 slice. The times are simulated.
32 devices in a mesh: dp: 8 (over z, y), tensor: 4 (over x, core).
Axes of the slice: x: 2, y: 2, z: 4, core: 2. Of those that a mesh axis runs over, the one named last changes fastest.
Arguments:
- tokens: bfloat16 [16384, 768], P('dp'), may hold values from -6 to 6
- w_query: bfloat16 [768, 768], P(None, 'tensor'), may hold values from -0.21875 to 0.21875
- w_key: bfloat16 [768, 768], P(None, 'tensor'), may hold values from -0.21875 to 0.21875
- w_value: bfloat16 [768, 768], P(None, 'tensor'), may hold values from -0.21875 to 0.21875
- b_query: float32 [768], P('tensor'), may hold values from -4 to 4
- b_value: float32 [768], P('tensor'), may hold values from -3 to 3
- conv_taps: float32 [12, 33], P('tensor'), may hold values from -0.3 to 0.3
- w_out: bfloat16 [768, 768], P('tensor'), may hold values from -0.875 to 0.875
- b_out: float32 [768], replicated, may hold values from -3 to 3
- gain_one: float32 [768], replicated, may hold values from 0.5 to 1.5
- shift_one: float32 [768], replicated, may hold values from -3 to 3
- w_up: bfloat16 [768, 3072], P(None, 'tensor'), may hold values from -0.21875 to 0.21875
- b_up: float32 [3072], P('tensor'), may hold values from -3 to 3
- w_down: bfloat16 [3072, 768], P('tensor'), may hold values from -0.109375 to 0.109375
- b_down: float32 [768], replicated, may hold values from -3 to 3
- gain_two: float32 [768], replicated, may hold values from 0.5 to 1.5
- shift_two: float32 [768], replicated, may hold values from -3 to 3
- cotangent: bfloat16 [16384, 768], P(('dp', 'tensor')), may hold values from -6 to 6
- segment_ids: int32 [16384], P('dp'), may hold values from 0 to 7, as said below
- landmark_ids: int32 [16384], P('dp'), may hold values from 0 to 63, as said below
Outputs:
- layer_out: bfloat16 [16384, 768], P(('dp', 'tensor'))
- input_grad: float32 [16384, 768], P(('dp', 'tensor'))
- grad_w_query: float32 [768, 768], P(None, 'tensor')
- grad_w_key: float32 [768, 768], P(None, 'tensor')
- grad_w_value: float32 [768, 768], P(None, 'tensor')
- grad_b_query: float32 [768], P('tensor')
- grad_b_value: float32 [768], P('tensor')
- grad_conv: float32 [12, 33], P('tensor')
- grad_w_out: float32 [768, 768], P('tensor')
- grad_b_out: float32 [768], replicated
- grad_gain_one: float32 [768], replicated
- grad_shift_one: float32 [768], replicated
- grad_w_up: float32 [768, 3072], P(None, 'tensor')
- grad_b_up: float32 [3072], P('tensor')
- grad_w_down: float32 [3072, 768], P('tensor')
- grad_b_down: float32 [768], replicated
- grad_gain_two: float32 [768], replicated
- grad_shift_two: float32 [768], replicated
Inputs may be any that keep to these rules, and one draw needn't show every extreme that they name: `segment_ids`: within each sequence of 1024 tokens the ids never fall and take every value from 0 to 7; every document holds 64 tokens or more. `landmark_ids`: within each sequence every id from 0 to 63 occurs, and the tokens with id j form one run inside document j // 8.
All inputs are finite; a program needn't handle non-finite values.
Results may differ from a plain program's by a relative error of at most 0.015.
Values may be sent and summed in bfloat16 or wider, within the bound.
No kernel may reach another device: no remote copies, remote signals or barrier semaphores. Data moves between devices by JAX's collectives and lax.ppermute only.
A program may use at most 256 MiB of HBM per device.

v0:
```python
import jax
import jax.numpy as jnp
from jax import lax
from jax.sharding import PartitionSpec as P

HEAD_DIM = 64
LANDMARKS = 64
CONV_TAPS = 33
PINV_STEPS = 6
DOCS = 8
SEQ_LEN = 1024
HIGH = lax.Precision.HIGHEST
EPSILON = 1e-05


def softmax_masked(scores, allowed):
    masked = jnp.where(allowed, scores, -1e30)
    highest = jnp.max(masked, axis=-1, keepdims=True)
    expo = jnp.exp(masked - highest)
    return expo / jnp.sum(expo, axis=-1, keepdims=True)


def layer_norm(inputs, scaling, offsets):
    centered = inputs - jnp.mean(inputs, axis=-1, keepdims=True)
    variance = jnp.mean(centered * centered, axis=-1, keepdims=True)
    return centered * lax.rsqrt(variance + EPSILON) * scaling + offsets


def gelu_exact(inputs):
    return jax.nn.gelu(inputs, approximate=False)


def nystrom(queries, key_rows, values, conv_weights, segment, landmark):
    row_count = queries.shape[0]
    head_count = queries.shape[1]
    score_scale = queries.shape[2] ** (-0.5)
    one_hot = (landmark[None, :] == jnp.arange(LANDMARKS, dtype=jnp.int32)[:, None]).astype(
        queries.dtype
    )
    pooling = one_hot / jnp.sum(one_hot, axis=1, keepdims=True)
    land_doc = jnp.arange(LANDMARKS, dtype=jnp.int32) // (LANDMARKS // DOCS)
    near_mask = segment[:, None] == land_doc[None, :]
    mark_mask = land_doc[:, None] == land_doc[None, :]
    key_marks = jnp.einsum("jt,the->jhe", pooling, key_rows, precision=HIGH)
    query_marks = jnp.einsum("jt,the->jhe", pooling, queries, precision=HIGH)
    kernel_one = softmax_masked(
        jnp.einsum("the,jhe->htj", queries, key_marks, precision=HIGH) * score_scale,
        near_mask[None],
    )
    middle = softmax_masked(
        jnp.einsum("ihe,jhe->hij", query_marks, key_marks, precision=HIGH) * score_scale,
        mark_mask[None],
    )
    kernel_last = softmax_masked(
        jnp.einsum("jhe,the->hjt", query_marks, key_rows, precision=HIGH) * score_scale,
        near_mask.T[None],
    )
    column_most = jnp.max(jnp.sum(middle, axis=1), axis=1)
    row_most = jnp.max(jnp.sum(middle, axis=2), axis=1)
    inverse = jnp.swapaxes(middle, 1, 2) / (column_most * row_most)[:, None, None]
    identity = jnp.eye(LANDMARKS, dtype=middle.dtype)
    for sweep in range(PINV_STEPS):
        product = jnp.einsum("hij,hjk->hik", middle, inverse, precision=HIGH)
        inner_term = 7.0 * identity - product
        inner_term = 15.0 * identity - jnp.einsum(
            "hij,hjk->hik", product, inner_term, precision=HIGH
        )
        inner_term = 13.0 * identity - jnp.einsum(
            "hij,hjk->hik", product, inner_term, precision=HIGH
        )
        inverse = 0.25 * jnp.einsum("hij,hjk->hik", inverse, inner_term, precision=HIGH)
    context = jnp.einsum("hjt,the->hje", kernel_last, values, precision=HIGH)
    blended = jnp.einsum("hij,hje->hie", inverse, context, precision=HIGH)
    attended = jnp.einsum("htj,hje->the", kernel_one, blended, precision=HIGH)
    half_width = CONV_TAPS // 2
    padded = jnp.pad(values, ((half_width, half_width), (0, 0), (0, 0)))
    seg_pad = jnp.pad(segment, (half_width, half_width), constant_values=-1)
    for offset in range(CONV_TAPS):
        same_doc = (seg_pad[offset : offset + row_count] == segment).astype(values.dtype)
        attended = (
            attended
            + conv_weights[:, offset][None, :, None]
            * padded[offset : offset + row_count]
            * same_doc[:, None, None]
        )
    return attended.reshape(row_count, head_count * values.shape[2])


def contract_rows(left, right):
    return lax.dot_general(
        left, right, (((0,), (0,)), ((), ())), preferred_element_type=jnp.float32
    )


def contract_cols(left, right):
    return lax.dot_general(
        left, right, (((1,), (1,)), ((), ())), preferred_element_type=jnp.float32
    )


def per_device(
    tokens,
    w_query,
    w_key,
    w_value,
    b_query,
    b_value,
    conv_taps,
    w_out,
    b_out,
    gain_one,
    shift_one,
    w_up,
    b_up,
    w_down,
    b_down,
    gain_two,
    shift_two,
    cotangent,
    segment_ids,
    landmark_ids,
):
    share_rows = tokens.shape[0] // lax.axis_size("tensor")
    first_row = lax.axis_index("tensor") * share_rows
    local_dim = w_query.shape[1]
    head_count = local_dim // HEAD_DIM
    seq_count = tokens.shape[0] // SEQ_LEN
    shaped = (seq_count, SEQ_LEN, head_count, HEAD_DIM)
    segments = segment_ids.reshape(seq_count, SEQ_LEN)
    marks = landmark_ids.reshape(seq_count, SEQ_LEN)
    queries = (jnp.dot(tokens, w_query, preferred_element_type=jnp.float32) + b_query).astype(
        jnp.bfloat16
    )
    key_rows = jnp.dot(tokens, w_key, preferred_element_type=jnp.float32).astype(jnp.bfloat16)
    values = (jnp.dot(tokens, w_value, preferred_element_type=jnp.float32) + b_value).astype(
        jnp.bfloat16
    )
    float_query = queries.astype(jnp.float32).reshape(shaped)
    float_key = key_rows.astype(jnp.float32).reshape(shaped)
    float_value = values.astype(jnp.float32).reshape(shaped)

    def attend(query_all, key_all, value_all, weights):
        return jax.vmap(nystrom, in_axes=(0, 0, 0, None, 0, 0))(
            query_all, key_all, value_all, weights, segments, marks
        )

    attended_f, attend_back = jax.vjp(attend, float_query, float_key, float_value, conv_taps)
    attended = attended_f.reshape(tokens.shape[0], local_dim).astype(jnp.bfloat16)
    summed = lax.psum_scatter(
        jnp.dot(attended, w_out, preferred_element_type=jnp.float32),
        "tensor",
        scatter_dimension=0,
        tiled=True,
    )
    own_tokens = lax.dynamic_slice_in_dim(tokens, first_row, share_rows, 0).astype(jnp.float32)
    normed, norm_back_one = jax.vjp(layer_norm, own_tokens + summed + b_out, gain_one, shift_one)
    normed_low = lax.all_gather(normed.astype(jnp.bfloat16), "tensor", axis=0, tiled=True)
    hidden = jnp.dot(normed_low, w_up, preferred_element_type=jnp.float32) + b_up
    activated_f, gelu_back = jax.vjp(gelu_exact, hidden)
    activated = activated_f.astype(jnp.bfloat16)
    branch = lax.psum_scatter(
        jnp.dot(activated, w_down, preferred_element_type=jnp.float32),
        "tensor",
        scatter_dimension=0,
        tiled=True,
    )
    output, norm_back_two = jax.vjp(layer_norm, normed + branch + b_down, gain_two, shift_two)
    grad_pre_out, grad_gain_two, grad_shift_two = norm_back_two(cotangent.astype(jnp.float32))
    grad_b_down = jnp.sum(grad_pre_out, axis=0)
    grad_branch = lax.all_gather(grad_pre_out.astype(jnp.bfloat16), "tensor", axis=0, tiled=True)
    grad_w_down = contract_rows(activated, grad_branch)
    grad_act = contract_cols(grad_branch, w_down)
    grad_hidden = gelu_back(grad_act)[0].astype(jnp.bfloat16)
    grad_w_up = contract_rows(normed_low, grad_hidden)
    grad_b_up = jnp.sum(grad_hidden, axis=0, dtype=jnp.float32)
    back_normed = lax.psum_scatter(
        contract_cols(grad_hidden, w_up).astype(jnp.bfloat16),
        "tensor",
        scatter_dimension=0,
        tiled=True,
    ).astype(jnp.float32)
    back_normed = lax.optimization_barrier(back_normed.astype(jnp.bfloat16)).astype(jnp.float32)
    grad_pre_norm, grad_gain_one, grad_shift_one = norm_back_one(grad_pre_out + back_normed)
    grad_b_out = jnp.sum(grad_pre_norm, axis=0)
    grad_summed = lax.all_gather(grad_pre_norm.astype(jnp.bfloat16), "tensor", axis=0, tiled=True)
    grad_w_out = contract_rows(attended, grad_summed)
    grad_attended = contract_cols(grad_summed, w_out).reshape(seq_count, SEQ_LEN, local_dim)
    grad_q_f, grad_k_f, grad_v_f, grad_conv = attend_back(grad_attended)
    grad_queries = grad_q_f.reshape(tokens.shape[0], local_dim).astype(jnp.bfloat16)
    grad_keys = grad_k_f.reshape(tokens.shape[0], local_dim).astype(jnp.bfloat16)
    grad_values = grad_v_f.reshape(tokens.shape[0], local_dim).astype(jnp.bfloat16)
    grad_w_query = contract_rows(tokens, grad_queries)
    grad_w_key = contract_rows(tokens, grad_keys)
    grad_w_value = contract_rows(tokens, grad_values)
    grad_b_query = jnp.sum(grad_queries, axis=0, dtype=jnp.float32)
    grad_b_value = jnp.sum(grad_values, axis=0, dtype=jnp.float32)
    total = contract_cols(grad_queries, w_query)
    total = total + contract_cols(grad_keys, w_key)
    input_grad = grad_pre_norm + lax.psum_scatter(
        (total + contract_cols(grad_values, w_value)).astype(jnp.bfloat16),
        "tensor",
        scatter_dimension=0,
        tiled=True,
    ).astype(jnp.float32)
    (
        grad_w_query,
        grad_w_key,
        grad_w_value,
        grad_b_query,
        grad_b_value,
        grad_conv,
        grad_w_out,
        grad_w_up,
        grad_w_down,
        grad_b_up,
    ) = lax.psum(
        (
            grad_w_query,
            grad_w_key,
            grad_w_value,
            grad_b_query,
            grad_b_value,
            grad_conv,
            grad_w_out,
            grad_w_up,
            grad_w_down,
            grad_b_up,
        ),
        "dp",
    )
    grad_gain_one, grad_shift_one, grad_b_out, grad_gain_two, grad_shift_two, grad_b_down = (
        lax.psum(
            (grad_gain_one, grad_shift_one, grad_b_out, grad_gain_two, grad_shift_two, grad_b_down),
            ("dp", "tensor"),
        )
    )
    return (
        output.astype(jnp.bfloat16),
        input_grad,
        grad_w_query,
        grad_w_key,
        grad_w_value,
        grad_b_query,
        grad_b_value,
        grad_conv,
        grad_w_out,
        grad_b_out,
        grad_gain_one,
        grad_shift_one,
        grad_w_up,
        grad_b_up,
        grad_w_down,
        grad_b_down,
        grad_gain_two,
        grad_shift_two,
    )


def solution(mesh):
    return jax.shard_map(
        per_device,
        mesh=mesh,
        in_specs=(
            P("dp", None),
            P(None, "tensor"),
            P(None, "tensor"),
            P(None, "tensor"),
            P("tensor"),
            P("tensor"),
            P("tensor", None),
            P("tensor", None),
            P(),
            P(),
            P(),
            P(None, "tensor"),
            P("tensor"),
            P("tensor", None),
            P(),
            P(),
            P(),
            P(("dp", "tensor"), None),
            P("dp"),
            P("dp"),
        ),
        out_specs=(
            P(("dp", "tensor"), None),
            P(("dp", "tensor"), None),
            P(None, "tensor"),
            P(None, "tensor"),
            P(None, "tensor"),
            P("tensor"),
            P("tensor"),
            P("tensor", None),
            P("tensor", None),
            P(),
            P(),
            P(),
            P(None, "tensor"),
            P("tensor"),
            P("tensor", None),
            P(),
            P(),
            P(),
        ),
        check_vma=False,
    )
```

profile of v0, /device:TPU:0, one launch (start us, length us, event | category | flops | bytes accessed | tf_op | source)
XLA Modules:
  0.0 814.8 jit_solution(1764736523739853846)
XLA Ops:
  28.8 4.2 convolution_convert_fusion.1
  61.8 16.0 %add_convert_fusion.3 = bf16[2,1024,3,64]{1,3,2,0:T(8,128)(2,1)S(1)} fusion(f32[2,1024,3,64]{1,3,2,0:T(8,128)S(1)} %copy.171, f32[2,3,64,64]{3,2,1,0:T(8,128)S(1)} %fusion.182, f32[2,1024]{1,0:T(2,128)S(1)} %copy-done.179, f32[3]{0:T(128)} %get-tuple-element.144, f32[2,1024]{1,0:T(2,128)S(1)} %copy-done.143, f32[3]{0:T(128)} %get-tuple-element.145, ...), kind=kOutput, calls=%fused_computation.126 | convolution fusion | flops 341704704 | bytes 4342156 | tf_op jit(solution)/shard_map/jvp(vmap(htj,hje->the))/dot_general | solution.py:74
  82.7 61.1 %reduce-scatter.5.cloned.1.call-done = f32[512,768]{1,0:T(8,128)} async-done(((f32[2048,768]{1,0:T(8,128)}), f32[512,768]{1,0:T(8,128)}) %reduce-scatter.5.cloned.1.call-update) | async-done | bytes 1572880 | tf_op jit(solution)/shard_map/reduce_scatter | solution.py:149
  147.7 28.6 %all-gather.4.cloned.1.call-done = bf16[2048,768]{1,0:T(8,128)(2,1)} async-done(((bf16[512,768]{1,0:T(8,128)(2,1)}), bf16[2048,768]{1,0:T(8,128)(2,1)}) %all-gather.4.cloned.1.call-update) | async-done | bytes 3145744 | tf_op jit(solution)/shard_map/all_gather | solution.py:157
  176.3 18.7 %multiply_convert_fusion = (bf16[2048,768]{1,0:T(8,128)(2,1)S(1)}, f32[2048,768]{1,0:T(8,128)}, f32[2048,768]{1,0:T(8,128)}) fusion(f32[768]{0:T(1024)S(1)} %copy-done.314, bf16[2048,768]{1,0:T(8,128)(2,1)} %all-gather.4.cloned.1.call-done, bf16[768,768]{1,0:T(8,128)(2,1)S(1)} %copy-done), kind=kOutput, calls=%fused_computation.5 | convolution fusion | flops 2519728128 | bytes 20057088 | tf_op jit(solution)/shard_map/dot_general | solution.py:158
  196.7 4.5 fusion.184
  201.2 58.5 %reduce-scatter.7.cloned.1.call-done = f32[512,768]{1,0:T(8,128)} async-done(((f32[2048,768]{1,0:T(8,128)}), f32[512,768]{1,0:T(8,128)}) %reduce-scatter.7.cloned.1.call-update) | async-done | bytes 1572880 | tf_op jit(solution)/shard_map/reduce_scatter | solution.py:161
  268.7 28.7 %all-gather.6.cloned.1.call-done = bf16[2048,768]{1,0:T(8,128)(2,1)} async-done(((bf16[512,768]{1,0:T(8,128)(2,1)}), bf16[2048,768]{1,0:T(8,128)(2,1)}) %all-gather.6.cloned.1.call-update) | async-done | bytes 3145744 | tf_op jit(solution)/shard_map/all_gather | solution.py:170
  297.3 11.1 %convert_reduce_fusion = (f32[768]{0:T(1024)}, bf16[2048,768]{1,0:T(8,128)(2,1)S(1)}) fusion(f32[2048,768]{1,0:T(8,128)} %get-tuple-element.189, f32[2048,768]{1,0:T(8,128)} %get-tuple-element.276, f32[768]{0:T(1024)S(1)} %copy-done.314, bf16[2048,768]{1,0:T(8,128)(2,1)} %all-gather.6.cloned.1.call-done, bf16[768,768]{1,0:T(8,128)(2,1)} %param.33), kind=kOutput, calls=%fused_computation.2 | convolution fusion | flops 2442657024 | bytes 20060160 | tf_op jit(solution)/shard_map/dot_general | solution.py:96
  314.2 38.1 %reduce-scatter.9.cloned.1.call-done = bf16[512,768]{1,0:T(8,128)(2,1)} async-done(((bf16[2048,768]{1,0:T(8,128)(2,1)}), bf16[512,768]{1,0:T(8,128)(2,1)}) %reduce-scatter.9.cloned.1.call-update) | async-done | bytes 786448 | tf_op jit(solution)/shard_map/reduce_scatter | solution.py:176
  365.6 25.1 %all-gather.8.cloned.1.call-done = bf16[2048,768]{1,0:T(8,128)(2,1)} async-done(((bf16[512,768]{1,0:T(8,128)(2,1)}), bf16[2048,768]{1,0:T(8,128)(2,1)}) %all-gather.8.cloned.1.call-update) | async-done | bytes 3145744 | tf_op jit(solution)/shard_map/all_gather | solution.py:185
  419.8 6.4 multiply_reduce_fusion.30
  426.3 5.1 multiply_multiply_fusion.17
  431.7 6.3 multiply_multiply_fusion.36
  438.2 5.6 multiply_multiply_fusion.26
  483.8 20.5 %pad_add_fusion = f32[2,1056,3,64]{1,3,2,0:T(8,128)} fusion(f32[2,1024,3,64]{1,3,2,0:T(8,128)} %get-tuple-element.229, f32[2,1024,3,64]{1,3,2,0:T(8,128)} %get-tuple-element.228, f32[2,1024,3,64]{1,3,2,0:T(8,128)} %get-tuple-element.227, f32[2,1024,3,64]{1,3,2,0:T(8,128)} %get-tuple-element.226, f32[2,1024,3,64]{1,3,2,0:T(8,128)} %get-tuple-element.225, ...), kind=kLoop, calls=%fused_computation.32 | loop fusion | flops 10543104 | bytes 44089344 | tf_op jit(solution)/shard_map/transpose(jvp(vmap()))/add_any | solution.py:83
  504.4 6.8 convert_reduce_fusion.2
  516.0 7.1 fusion.203
  523.1 4.2 fusion.202
  535.2 40.7 %all-reduce.68 = (f32[768]{0:T(1024)}, f32[768]{0:T(1024)}, f32[768]{0:T(1024)}, f32[768]{0:T(1024)}, f32[768]{0:T(1024)}, /*index=5*/f32[768]{0:T(1024)}) all-reduce(f32[768]{0:T(1024)S(1)} %copy-done.242, f32[768]{0:T(1024)S(1)} %copy-done.252, f32[768]{0:T(1024)S(1)} %copy-done.253, ...), channel_id=1, replica_groups=mesh['dp'=8,'tensor'=4] {'dp','tensor'}, use_global_device_ids=true, to_apply=%region_79.80 | all-reduce | flops 4608 | bytes 36864 | tf_op jit(solution)/shard_map/psum | solution.py:232
  580.6 4.0 multiply_reduce_fusion.32
  584.8 4.0 multiply_reduce_fusion.33
  589.0 39.9 %all-reduce.69 = (f32[192]{0:T(256)}, f32[192]{0:T(256)}, f32[3,33]{0,1:T(8,128)S(1)}, f32[768]{0:T(1024)}) all-reduce(f32[192]{0:T(256)S(1)} %reduce_sum.660, f32[192]{0:T(256)S(1)} %reduce_sum.665, f32[3,33]{0,1:T(8,128)S(1)} %pad_add_fusion.7, f32[768]{0:T(1024)S(1)} %copy-done.268), channel_id=1, replica_groups=mesh['dp'=8,'tensor'=4] {'dp'}, use_global_device_ids=true, to_apply=%region_39.40 | all-reduce | flops 1251 | bytes 10008 | tf_op jit(solution)/shard_map/psum | solution.py:216
  632.5 166.6 %all-reduce.73.cloned.1.call-done = (f32[768,192]{0,1:T(8,128)}, f32[768,192]{0,1:T(8,128)}, f32[768,192]{0,1:T(8,128)}, f32[192,768]{1,0:T(8,128)}, f32[768,768]{1,0:T(8,128)}, /*index=5*/f32[768,768]{1,0:T(8,128)}) async-done(((f32[768,192]{0,1:T(8,128)}, f32[768,192]{0,1:T(8,128)}, f32[768,192]{0,1:T(8,128)}, f32[192,768]{1,0:T(8,128)}, f32[768,768]{1,0:T(8,128)}, /*index=5*/f32[768,768]{1,0:T(8,128)}), ...) | async-done | bytes 7077904 | tf_op jit(solution)/shard_map/psum | solution.py:216
  (852 shorter events, 183.6 us)
Async XLA Ops:
  7.2 169.1 %copy-start = (bf16[768,768]{1,0:T(8,128)(2,1)S(1)}, bf16[768,768]{1,0:T(8,128)(2,1)}, u32[]{:S(2)}) copy-start(bf16[768,768]{1,0:T(8,128)(2,1)} %param.31) | copy-start | bytes 3538948
  7.2 136.6 %reduce-scatter.5.cloned.1.call-start = ((), (), s32[]{:S(2)}) async-start(), calls=%async_computation.4 | async-start | bytes 7864320 | tf_op jit(solution)/shard_map/reduce_scatter | solution.py:149
  61.4 303.6 %copy-start.116 = (f32[2,3,1024]{2,1,0:T(4,128)}, f32[2,3,1024]{2,1,0:T(4,128)S(1)}, u32[]{:S(2)}) copy-start(f32[2,3,1024]{2,1,0:T(4,128)S(1)} %fusion.65) | copy-start | bytes 73732
  82.6 61.2 %copy-start.259 = (f32[768]{0:T(1024)S(1)}, f32[768]{0:T(1024)}, u32[]{:S(2)}) copy-start(f32[768]{0:T(1024)} %param.28) | copy-start | bytes 9220
  82.6 93.7 %all-gather.4.cloned.1.call-start = ((), (), s32[]{:S(2)}) async-start(), calls=%async_computation.5 | async-start | bytes 3932160 | tf_op jit(solution)/shard_map/all_gather | solution.py:157
  147.6 112.1 %reduce-scatter.7.cloned.1.call-start = ((), (), s32[]{:S(2)}) async-start(), calls=%async_computation.6 | async-start | bytes 7864320 | tf_op jit(solution)/shard_map/reduce_scatter | solution.py:161
  201.2 58.5 %copy-start.269 = (f32[768]{0:T(1024)S(1)}, f32[768]{0:T(1024)}, u32[]{:S(2)}) copy-start(f32[768]{0:T(1024)} %param.34) | copy-start | bytes 9220
  201.2 96.2 %all-gather.6.cloned.1.call-start = ((), (), s32[]{:S(2)}) async-start(), calls=%async_computation.7 | async-start | bytes 3932160 | tf_op jit(solution)/shard_map/all_gather | solution.py:170
  268.6 83.6 %reduce-scatter.9.cloned.1.call-start = ((), (), s32[]{:S(2)}) async-start(), calls=%async_computation.8 | async-start | bytes 3932160 | tf_op jit(solution)/shard_map/reduce_scatter | solution.py:176
  314.1 76.6 %all-gather.8.cloned.1.call-start = ((), (), s32[]{:S(2)}) async-start(), calls=%async_computation.9 | async-start | bytes 3932160 | tf_op jit(solution)/shard_map/all_gather | solution.py:185
  362.1 267.4 %reduce-scatter.11.cloned.1.call-start = ((), (), s32[]{:S(2)}) async-start(), calls=%async_computation.10 | async-start | bytes 3932160 | tf_op jit(solution)/shard_map/reduce_scatter | solution.py:199
  400.3 47.6 %copy-start.106 = (f32[2,3,64,64]{3,2,1,0:T(8,128)}, f32[2,3,64,64]{3,2,1,0:T(8,128)S(1)}, u32[]{:S(2)}) copy-start(f32[2,3,64,64]{3,2,1,0:T(8,128)S(1)} %fusion.185) | copy-start | bytes 294916
  516.0 283.2 %all-reduce.73.cloned.1.call-start = ((), (), s32[]{:S(2)}) async-start(), calls=%async_computation.11 | async-start | bytes 14155776 | tf_op jit(solution)/shard_map/psum | solution.py:216
  534.5 41.5 %copy-start.255 = (f32[3,64]{1,0:T(4,128)S(1)}, f32[3,64]{1,0:T(4,128)}, u32[]{:S(2)}) copy-start(f32[3,64]{1,0:T(4,128)} %get-tuple-element.283) | copy-start | bytes 2308
  534.5 41.8 %copy-start.148 = (f32[2,1024]{1,0:T(2,128)S(1)}, f32[2,1024]{1,0:T(2,128)}, u32[]{:S(2)}) copy-start(f32[2,1024]{1,0:T(2,128)} %get-tuple-element.244) | copy-start | bytes 24580
  534.5 41.8 %copy-start.151 = (f32[2,1024]{1,0:T(2,128)S(1)}, f32[2,1024]{1,0:T(2,128)}, u32[]{:S(2)}) copy-start(f32[2,1024]{1,0:T(2,128)} %get-tuple-element.245) | copy-start | bytes 24580
  534.5 41.8 %copy-start.154 = (f32[2,1024]{1,0:T(2,128)S(1)}, f32[2,1024]{1,0:T(2,128)}, u32[]{:S(2)}) copy-start(f32[2,1024]{1,0:T(2,128)} %get-tuple-element.246) | copy-start | bytes 24580
  534.5 41.8 %copy-start.157 = (f32[2,1024]{1,0:T(2,128)S(1)}, f32[2,1024]{1,0:T(2,128)}, u32[]{:S(2)}) copy-start(f32[2,1024]{1,0:T(2,128)} %get-tuple-element.247) | copy-start | bytes 24580
  534.6 41.8 %copy-start.160 = (f32[2,1024]{1,0:T(2,128)S(1)}, f32[2,1024]{1,0:T(2,128)}, u32[]{:S(2)}) copy-start(f32[2,1024]{1,0:T(2,128)} %get-tuple-element.248) | copy-start | bytes 24580
  534.6 41.8 %copy-start.163 = (f32[2,1024]{1,0:T(2,128)S(1)}, f32[2,1024]{1,0:T(2,128)}, u32[]{:S(2)}) copy-start(f32[2,1024]{1,0:T(2,128)} %get-tuple-element.249) | copy-start | bytes 24580
  534.6 41.8 %copy-start.166 = (f32[2,1024]{1,0:T(2,128)S(1)}, f32[2,1024]{1,0:T(2,128)}, u32[]{:S(2)}) copy-start(f32[2,1024]{1,0:T(2,128)} %get-tuple-element.236) | copy-start | bytes 24580
  534.6 41.8 %copy-start.169 = (f32[2,1024]{1,0:T(2,128)S(1)}, f32[2,1024]{1,0:T(2,128)}, u32[]{:S(2)}) copy-start(f32[2,1024]{1,0:T(2,128)} %get-tuple-element.241) | copy-start | bytes 24580
  534.6 41.8 %copy-start.172 = (f32[2,1024]{1,0:T(2,128)S(1)}, f32[2,1024]{1,0:T(2,128)}, u32[]{:S(2)}) copy-start(f32[2,1024]{1,0:T(2,128)} %get-tuple-element.242) | copy-start | bytes 24580
  584.8 44.7 %copy-start.237 = (f32[512]{0:T(512)S(1)}, f32[512]{0:T(512)}, u32[]{:S(2)}) copy-start(f32[512]{0:T(512)} %copy-done.236) | copy-start | bytes 6148
  (305 other events, 1261.9 us)
Sparse Core Ops, SparseCore 0:
  82.7 61.0 reduce-scatter.4
  147.7 28.5 all-gather.3
  201.3 58.3 reduce-scatter.6
  268.7 28.5 all-gather.5
  314.2 37.9 reduce-scatter.8
  362.2 28.5 all-gather.7
  516.1 38.6 reduce-scatter.10
  561.0 238.0 all-reduce.72
where the time goes:
time: 822 us; the launch traced here: 815 us
  waiting for transfers between devices  407 us (50%)
  matrix products  168 us (20%)
  other arithmetic  92.5 us (11%)
  blocking collectives  80.6 us (10%)
  local copies, waits for them, and re-layouts  46.4 us (6%)
  between operations  19.5 us (2%)
    psum x1, waiting for transfers between devices, per_device(): lax.psum((grad_w_query, grad_w_key, grad_w_value, grad_b_query, grad_b_va...  167 us
    reduce_scatter x1, waiting for transfers between devices, per_device(): lax.psum_scatter(jnp.dot(attended, w_out, preferred_element_type=jnp.floa...  61.1 us
    reduce_scatter x1, waiting for transfers between devices, per_device(): lax.psum_scatter(jnp.dot(activated, w_down, preferred_element_type=jnp.fl...  58.5 us
    psum x1, blocking collectives, per_device(): lax.psum((grad_gain_one, grad_shift_one, grad_b_out, grad_gain_two, grad_...  40.7 us
    psum x1, blocking collectives, per_device(): lax.psum((grad_w_query, grad_w_key, grad_w_value, grad_b_query, grad_b_va...  39.9 us
    reduce_scatter x1, waiting for transfers between devices, per_device(): lax.psum_scatter(contract_cols(grad_hidden, w_up).astype(jnp.bfloat16), '...  38.1 us
    dot_general x6, matrix products, contract_cols(): lax.dot_general(left, right, (((1,), (1,)), ((), ())), preferred_element_...  29 us
    all_gather x1, waiting for transfers between devices, per_device(): lax.all_gather(grad_pre_out.astype(jnp.bfloat16), 'tensor', axis=0, tiled...  28.7 us
  transfers between devices with their start and end apart: 8, of which 7 were waited for; matrix products, arithmetic and copies ran while one was open for 5% of the time, Pallas kernels for 0%

commit v1 on v0

--- a/solution.py
+++ b/solution.py
@@ -11,6 +11,24 @@
 SEQ_LEN = 1024
 HIGH = lax.Precision.HIGHEST
 EPSILON = 1e-05
+
+
+def ring_gather(shard, axis, dim):
+    ways, here, step = (lax.axis_size(axis), lax.axis_index(axis), shard.shape[dim])
+    shape = [n * ways if d == dim else n for d, n in enumerate(shard.shape)]
+    full = lax.dynamic_update_slice_in_dim(
+        jnp.zeros(shape, shard.dtype), shard, here * step, axis=dim
+    )
+    going_up = going_down = shard
+    for far in range(1, ways // 2 + 1):
+        going_up = lax.ppermute(going_up, axis, [(d, (d + 1) % ways) for d in range(ways)])
+        full = lax.dynamic_update_slice_in_dim(full, going_up, (here - far) % ways * step, axis=dim)
+        if 2 * far < ways:
+            going_down = lax.ppermute(going_down, axis, [(d, (d - 1) % ways) for d in range(ways)])
+            full = lax.dynamic_update_slice_in_dim(
+                full, going_down, (here + far) % ways * step, axis=dim
+            )
+    return full
 
 
 def softmax_masked(scores, allowed):
@@ -182,7 +200,7 @@
     back_normed = lax.optimization_barrier(back_normed.astype(jnp.bfloat16)).astype(jnp.float32)
     grad_pre_norm, grad_gain_one, grad_shift_one = norm_back_one(grad_pre_out + back_normed)
     grad_b_out = jnp.sum(grad_pre_norm, axis=0)
-    grad_summed = lax.all_gather(grad_pre_norm.astype(jnp.bfloat16), "tensor", axis=0, tiled=True)
+    grad_summed = ring_gather(grad_pre_norm.astype(jnp.bfloat16), "tensor", 0)
     grad_w_out = contract_rows(attended, grad_summed)
     grad_attended = contract_cols(grad_summed, w_out).reshape(seq_count, SEQ_LEN, local_dim)
     grad_q_f, grad_k_f, grad_v_f, grad_conv = attend_back(grad_attended)

time: 822 us -> 823 us (level)
    all_gather x1 -> x0, waiting for transfers between devices: 25.1 us -> none  [per_device(): lax.all_gather(grad_pre_norm.astype(jnp.bfloat16), 'tensor', axis=0, tile...]
    ppermute x0 -> x3, waiting for transfers between devices: none -> 21.9 us  [the longest x2 21.9 us: ring_gather(): lax.ppermute(going_up, axis, [(d, (d + 1) % ways) for d in range(ways)])]
    unnamed x653 -> x649, local copies, waits for them, and re-layouts: 24.1 us -> 25.1 us
  transfers between devices with their start and end apart: 8 -> 10, of which waited for: 7 -> 8; matrix products, arithmetic and copies ran while one was open for 5% -> 5% of each run, Pallas kernels for 0% -> 0%
where the time goes in v1:
time: 823 us; the launch traced here: 816 us
  waiting for transfers between devices  403 us (49%)
  matrix products  167 us (20%)
  other arithmetic  91 us (11%)
  blocking collectives  80.1 us (10%)
  local copies, waits for them, and re-layouts  52.4 us (6%)
  between operations  19.5 us (2%)
    psum x1, waiting for transfers between devices, per_device(): lax.psum((grad_w_query, grad_w_key, grad_w_value, grad_b_query, grad_b_va...  166 us
    reduce_scatter x1, waiting for transfers between devices, per_device(): lax.psum_scatter(jnp.dot(attended, w_out, preferred_element_type=jnp.floa...  61.1 us
    reduce_scatter x1, waiting for transfers between devices, per_device(): lax.psum_scatter(jnp.dot(activated, w_down, preferred_element_type=jnp.fl...  58.5 us
    psum x1, blocking collectives, per_device(): lax.psum((grad_gain_one, grad_shift_one, grad_b_out, grad_gain_two, grad_...  41.7 us
    psum x1, blocking collectives, per_device(): lax.psum((grad_w_query, grad_w_key, grad_w_value, grad_b_query, grad_b_va...  38.5 us
    reduce_scatter x1, waiting for transfers between devices, per_device(): lax.psum_scatter(contract_cols(grad_hidden, w_up).astype(jnp.bfloat16), '...  38.1 us
    all_gather x1, waiting for transfers between devices, per_device(): lax.all_gather(grad_pre_out.astype(jnp.bfloat16), 'tensor', axis=0, tiled...  28.7 us
    all_gather x1, waiting for transfers between devices, per_device(): lax.all_gather(normed.astype(jnp.bfloat16), 'tensor', axis=0, tiled=True)  28.6 us
  transfers between devices with their start and end apart: 10, of which 8 were waited for; matrix products, arithmetic and copies ran while one was open for 5% of the time, Pallas kernels for 0%

profile of v1, /device:TPU:0, one launch (start us, length us, event | category | flops | bytes accessed | tf_op | source)
XLA Modules:
  0.0 815.5 jit_solution(15090948292566080242)
XLA Ops:
  28.9 4.2 convolution_convert_fusion.1
  62.2 16.0 %add_convert_fusion.3 = bf16[2,1024,3,64]{1,3,2,0:T(8,128)(2,1)S(1)} fusion(f32[2,1024,3,64]{1,3,2,0:T(8,128)S(1)} %copy.171, f32[2,3,64,64]{3,2,1,0:T(8,128)S(1)} %fusion.182, f32[2,1024]{1,0:T(2,128)S(1)} %copy-done.182, f32[3]{0:T(128)} %get-tuple-element.144, f32[2,1024]{1,0:T(2,128)S(1)} %copy-done.146, f32[3]{0:T(128)} %get-tuple-element.145, ...), kind=kOutput, calls=%fused_computation.126 | convolution fusion | flops 341704704 | bytes 4342156 | tf_op jit(solution)/shard_map/jvp(vmap(htj,hje->the))/dot_general | solution.py:92
  83.0 61.1 %reduce-scatter.5.cloned.1.call-done = f32[512,768]{1,0:T(8,128)} async-done(((f32[2048,768]{1,0:T(8,128)}), f32[512,768]{1,0:T(8,128)}) %reduce-scatter.5.cloned.1.call-update) | async-done | bytes 1572880 | tf_op jit(solution)/shard_map/reduce_scatter | solution.py:167
  148.0 28.6 %all-gather.3.cloned.1.call-done = bf16[2048,768]{1,0:T(8,128)(2,1)} async-done(((bf16[512,768]{1,0:T(8,128)(2,1)}), bf16[2048,768]{1,0:T(8,128)(2,1)}) %all-gather.3.cloned.1.call-update) | async-done | bytes 3145744 | tf_op jit(solution)/shard_map/all_gather | solution.py:175
  176.7 18.7 %multiply_convert_fusion = (bf16[2048,768]{1,0:T(8,128)(2,1)S(1)}, f32[2048,768]{1,0:T(8,128)}, f32[2048,768]{1,0:T(8,128)}) fusion(f32[768]{0:T(1024)S(1)} %copy-done.312, bf16[2048,768]{1,0:T(8,128)(2,1)} %all-gather.3.cloned.1.call-done, bf16[768,768]{1,0:T(8,128)(2,1)S(1)} %copy-done), kind=kOutput, calls=%fused_computation.5 | convolution fusion | flops 2519728128 | bytes 20057088 | tf_op jit(solution)/shard_map/dot_general | solution.py:176
  197.0 4.5 fusion.184
  201.6 58.5 %reduce-scatter.7.cloned.1.call-done = f32[512,768]{1,0:T(8,128)} async-done(((f32[2048,768]{1,0:T(8,128)}), f32[512,768]{1,0:T(8,128)}) %reduce-scatter.7.cloned.1.call-update) | async-done | bytes 1572880 | tf_op jit(solution)/shard_map/reduce_scatter | solution.py:179
  269.0 28.7 %all-gather.5.cloned.1.call-done = bf16[2048,768]{1,0:T(8,128)(2,1)} async-done(((bf16[512,768]{1,0:T(8,128)(2,1)}), bf16[2048,768]{1,0:T(8,128)(2,1)}) %all-gather.5.cloned.1.call-update) | async-done | bytes 3145744 | tf_op jit(solution)/shard_map/all_gather | solution.py:188
  297.7 11.1 %convert_reduce_fusion = (f32[768]{0:T(1024)}, bf16[2048,768]{1,0:T(8,128)(2,1)S(1)}) fusion(f32[2048,768]{1,0:T(8,128)} %get-tuple-element.191, f32[2048,768]{1,0:T(8,128)} %get-tuple-element.278, f32[768]{0:T(1024)S(1)} %copy-done.312, bf16[2048,768]{1,0:T(8,128)(2,1)} %all-gather.5.cloned.1.call-done, bf16[768,768]{1,0:T(8,128)(2,1)} %param.33), kind=kOutput, calls=%fused_computation.2 | convolution fusion | flops 2442657024 | bytes 20060160 | tf_op jit(solution)/shard_map/dot_general | solution.py:114
  310.5 4.4 convolution_convert_fusion
  314.9 38.1 %reduce-scatter.9.cloned.1.call-done = bf16[512,768]{1,0:T(8,128)(2,1)} async-done(((bf16[2048,768]{1,0:T(8,128)(2,1)}), bf16[512,768]{1,0:T(8,128)(2,1)}) %reduce-scatter.9.cloned.1.call-update) | async-done | bytes 786448 | tf_op jit(solution)/shard_map/reduce_scatter | solution.py:194
  362.5 16.6 %collective-permute-done = bf16[512,768]{1,0:T(8,128)(2,1)} collective-permute-done((bf16[512,768]{1,0:T(8,128)(2,1)}, bf16[512,768]{1,0:T(8,128)(2,1)}, u32[]{:S(2)}, u32[]{:S(2)}) %collective-permute-start) | collective-permute-done | bytes 786464 | tf_op jit(solution)/shard_map/ppermute | solution.py:24
  385.5 5.3 collective-permute-done.2
  421.0 6.3 multiply_reduce_fusion.30
  427.5 5.1 multiply_multiply_fusion.17
  432.9 6.3 multiply_multiply_fusion.36
  439.4 5.6 multiply_multiply_fusion.26
  485.0 20.5 %pad_add_fusion = f32[2,1056,3,64]{1,3,2,0:T(8,128)} fusion(f32[2,1024,3,64]{1,3,2,0:T(8,128)} %get-tuple-element.231, f32[2,1024,3,64]{1,3,2,0:T(8,128)} %get-tuple-element.230, f32[2,1024,3,64]{1,3,2,0:T(8,128)} %get-tuple-element.229, f32[2,1024,3,64]{1,3,2,0:T(8,128)} %get-tuple-element.228, f32[2,1024,3,64]{1,3,2,0:T(8,128)} %get-tuple-element.227, ...), kind=kLoop, calls=%fused_computation.32 | loop fusion | flops 10543104 | bytes 44089344 | tf_op jit(solution)/shard_map/transpose(jvp(vmap()))/add_any | solution.py:101
  505.6 6.8 convert_reduce_fusion.2
  517.2 7.1 fusion.203
  536.8 4.2 multiply_reduce_fusion.31
  549.5 38.5 %all-reduce.69 = (f32[192]{0:T(256)}, f32[192]{0:T(256)}, f32[3,33]{0,1:T(8,128)S(1)}, f32[768]{0:T(1024)}) all-reduce(f32[192]{0:T(256)S(1)} %reduce_sum.660, f32[192]{0:T(256)S(1)} %reduce_sum.665, f32[3,33]{0,1:T(8,128)S(1)} %pad_add_fusion.7, f32[768]{0:T(1024)S(1)} %copy-done.266), channel_id=1, replica_groups=mesh['dp'=8,'tensor'=4] {'dp'}, use_global_device_ids=true, to_apply=%region_39.40 | all-reduce | flops 1251 | bytes 10008 | tf_op jit(solution)/shard_map/psum | solution.py:234
  591.8 41.7 %all-reduce.68 = (f32[768]{0:T(1024)}, f32[768]{0:T(1024)}, f32[768]{0:T(1024)}, f32[768]{0:T(1024)}, f32[768]{0:T(1024)}, /*index=5*/f32[768]{0:T(1024)}) all-reduce(f32[768]{0:T(1024)S(1)} %get-tuple-element.203, f32[768]{0:T(1024)S(1)} %copy-done.250, ...), channel_id=1, replica_groups=mesh['dp'=8,'tensor'=4] {'dp','tensor'}, use_global_device_ids=true, to_apply=%region_79.80 | all-reduce | flops 4608 | bytes 36864 | tf_op jit(solution)/shard_map/psum | solution.py:250
  633.4 166.4 %all-reduce.73.cloned.1.call-done = (f32[768,192]{0,1:T(8,128)}, f32[768,192]{0,1:T(8,128)}, f32[768,192]{0,1:T(8,128)}, f32[192,768]{1,0:T(8,128)}, f32[768,768]{1,0:T(8,128)}, /*index=5*/f32[768,768]{1,0:T(8,128)}) async-done(((f32[768,192]{0,1:T(8,128)}, f32[768,192]{0,1:T(8,128)}, f32[768,192]{0,1:T(8,128)}, f32[192,768]{1,0:T(8,128)}, f32[768,768]{1,0:T(8,128)}, /*index=5*/f32[768,768]{1,0:T(8,128)}), ...) | async-done | bytes 7077904 | tf_op jit(solution)/shard_map/psum | solution.py:234
  (855 shorter events, 191.9 us)
Async XLA Ops:
  7.2 169.5 %copy-start = (bf16[768,768]{1,0:T(8,128)(2,1)S(1)}, bf16[768,768]{1,0:T(8,128)(2,1)}, u32[]{:S(2)}) copy-start(bf16[768,768]{1,0:T(8,128)(2,1)} %param.31) | copy-start | bytes 3538948
  7.2 137.0 %reduce-scatter.5.cloned.1.call-start = ((), (), s32[]{:S(2)}) async-start(), calls=%async_computation.4 | async-start | bytes 7864320 | tf_op jit(solution)/shard_map/reduce_scatter | solution.py:167
  11.9 37.7 %copy-start.91 = (f32[64,64]{1,0:T(8,128)}, f32[64,64]{1,0:T(8,128)S(1)}, u32[]{:S(2)}) copy-start(f32[64,64]{1,0:T(8,128)S(1)} %fusion.149) | copy-start | bytes 49156
  11.9 37.3 %copy-start.39 = (f32[64,64]{1,0:T(8,128)}, f32[64,64]{1,0:T(8,128)S(1)}, u32[]{:S(2)}) copy-start(f32[64,64]{1,0:T(8,128)S(1)} %get-tuple-element.293) | copy-start | bytes 49156
  11.9 37.3 %copy-start.93 = (f32[64,64]{1,0:T(8,128)}, f32[64,64]{1,0:T(8,128)S(1)}, u32[]{:S(2)}) copy-start(f32[64,64]{1,0:T(8,128)S(1)} %get-tuple-element.294) | copy-start | bytes 49156
  82.9 61.2 %copy-start.257 = (f32[768]{0:T(1024)S(1)}, f32[768]{0:T(1024)}, u32[]{:S(2)}) copy-start(f32[768]{0:T(1024)} %param.28) | copy-start | bytes 9220
  83.0 93.7 %all-gather.3.cloned.1.call-start = ((), (), s32[]{:S(2)}) async-start(), calls=%async_computation.5 | async-start | bytes 3932160 | tf_op jit(solution)/shard_map/all_gather | solution.py:175
  146.8 29.9 %copy-start.312 = (f32[768]{0:T(1024)S(1)}, f32[768]{0:T(1024)}, u32[]{:S(2)}) copy-start(f32[768]{0:T(1024)} %param.32) | copy-start | bytes 9220
  148.0 112.1 %reduce-scatter.7.cloned.1.call-start = ((), (), s32[]{:S(2)}) async-start(), calls=%async_computation.6 | async-start | bytes 7864320 | tf_op jit(solution)/shard_map/reduce_scatter | solution.py:179
  176.7 20.4 %copy-start.311 = (bf16[768,768]{1,0:T(8,128)(2,1)S(1)}, bf16[768,768]{1,0:T(8,128)(2,1)}, u32[]{:S(2)}) copy-start(bf16[768,768]{1,0:T(8,128)(2,1)} %param.33) | copy-start | bytes 3538948
  201.5 58.5 %copy-start.267 = (f32[768]{0:T(1024)S(1)}, f32[768]{0:T(1024)}, u32[]{:S(2)}) copy-start(f32[768]{0:T(1024)} %param.34) | copy-start | bytes 9220
  201.5 96.2 %all-gather.5.cloned.1.call-start = ((), (), s32[]{:S(2)}) async-start(), calls=%async_computation.7 | async-start | bytes 3932160 | tf_op jit(solution)/shard_map/all_gather | solution.py:188
  269.0 84.0 %reduce-scatter.9.cloned.1.call-start = ((), (), s32[]{:S(2)}) async-start(), calls=%async_computation.8 | async-start | bytes 3932160 | tf_op jit(solution)/shard_map/reduce_scatter | solution.py:194
  314.9 273.8 %reduce-scatter.11.cloned.1.call-start = ((), (), s32[]{:S(2)}) async-start(), calls=%async_computation.9 | async-start | bytes 3932160 | tf_op jit(solution)/shard_map/reduce_scatter | solution.py:217
  360.2 18.9 %collective-permute-start = (bf16[512,768]{1,0:T(8,128)(2,1)}, bf16[512,768]{1,0:T(8,128)(2,1)}, u32[]{:S(2)}, u32[]{:S(2)}) collective-permute-start(bf16[512,768]{1,0:T(8,128)(2,1)} %get-tuple-element.183), channel_id=1, source_target_pairs={{0,1},{1,2},{2,3},{3,0},{4,5},{5,6},{6,7},{7,4},{8,9},{9,10},{10,1... | collective-permute-start | bytes 2359304 | tf_op jit(solution)/shard_map/ppermute | solution.py:24
  360.8 23.5 %collective-permute-start.1 = (bf16[512,768]{1,0:T(8,128)(2,1)}, bf16[512,768]{1,0:T(8,128)(2,1)}, u32[]{:S(2)}, u32[]{:S(2)}) collective-permute-start(bf16[512,768]{1,0:T(8,128)(2,1)} %get-tuple-element.183), channel_id=1, source_target_pairs={{0,3},{1,0},{2,1},{3,2},{4,7},{5,4},{6,5},{7,6},{8,11},{9,8},{10,9... | collective-permute-start | bytes 2359304 | tf_op jit(solution)/shard_map/ppermute | solution.py:27
  379.1 11.7 %collective-permute-start.2 = (bf16[512,768]{1,0:T(8,128)(2,1)}, bf16[512,768]{1,0:T(8,128)(2,1)}, u32[]{:S(2)}, u32[]{:S(2)}) collective-permute-start(bf16[512,768]{1,0:T(8,128)(2,1)} %collective-permute-done), channel_id=1, source_target_pairs={{0,1},{1,2},{2,3},{3,0},{4,5},{5,6},{6,7},{7,4},{8,9},{9,10},{10,1... | collective-permute-start | bytes 2359304 | tf_op jit(solution)/shard_map/ppermute | solution.py:24
  401.5 47.6 %copy-start.109 = (f32[2,3,64,64]{3,2,1,0:T(8,128)}, f32[2,3,64,64]{3,2,1,0:T(8,128)S(1)}, u32[]{:S(2)}) copy-start(f32[2,3,64,64]{3,2,1,0:T(8,128)S(1)} %fusion.185) | copy-start | bytes 294916
  485.0 20.5 %copy-start.10 = (f32[2,3,64,1024]{3,2,1,0:T(8,128)S(1)}, f32[2,3,64,1024]{3,2,1,0:T(8,128)}, u32[]{:S(2)}) copy-start(f32[2,3,64,1024]{3,2,1,0:T(8,128)} %copy-done.8) | copy-start | bytes 4718596
  485.0 20.6 %copy-start.110 = (f32[2,3,64,64]{3,2,1,0:T(8,128)S(1)}, f32[2,3,64,64]{3,2,1,0:T(8,128)}, u32[]{:S(2)}) copy-start(f32[2,3,64,64]{3,2,1,0:T(8,128)} %copy-done.109) | copy-start | bytes 294916
  485.0 20.6 %copy-start.211 = (f32[2,3,64]{2,1,0:T(4,128)S(1)}, f32[2,3,64]{2,1,0:T(4,128)}, u32[]{:S(2)}) copy-start(f32[2,3,64]{2,1,0:T(4,128)} %copy-done.209) | copy-start | bytes 4612
  485.0 20.6 %copy-start.215 = (f32[2,3,64]{2,1,0:T(4,128)S(1)}, f32[2,3,64]{2,1,0:T(4,128)}, u32[]{:S(2)}) copy-start(f32[2,3,64]{2,1,0:T(4,128)} %copy-done.212) | copy-start | bytes 4612
  517.1 282.7 %all-reduce.73.cloned.1.call-start = ((), (), s32[]{:S(2)}) async-start(), calls=%async_computation.10 | async-start | bytes 14155776 | tf_op jit(solution)/shard_map/psum | solution.py:234
  545.4 43.3 %copy-start.238 = (f32[512]{0:T(512)S(1)}, f32[512]{0:T(512)}, u32[]{:S(2)}) copy-start(f32[512]{0:T(512)} %copy-done.237) | copy-start | bytes 6148
  (305 other events, 967.3 us)
Sparse Core Ops, SparseCore 0:
  83.1 61.0 reduce-scatter.4
  148.1 28.5 all-gather.2
  201.7 58.3 reduce-scatter.6
  269.1 28.5 all-gather.4
  315.0 37.9 reduce-scatter.8
  517.2 37.6 reduce-scatter.10
  561.2 238.5 all-reduce.72
